TPU v7x, 32 devices: a whole 2x2x4 slice. The times are simulated.
32 devices in a mesh: chain: 16 (over z, y, core), aux: 2 (over x).
Axes of the slice: x: 2, y: 2, z: 4, core: 2. Of those that a mesh axis runs over, the one named last changes fastest.
Arguments:
- occupied: bfloat16 [2048, 1152], P('chain'), may hold values from -0.1875 to 0.1875
- virtual: bfloat16 [2048, 1152], P('chain'), may hold values from -0.1875 to 0.1875
- three_centre: bfloat16 [32, 2048, 1152], P('aux', 'chain'), may hold values from -6 to 6
- kernel: bfloat16 [32, 32], P('aux'), may hold values from -1 to 1
- profile: int32 [16], replicated, may hold values from 2 to 4
- atom_map: int32 [32], P('aux'), may hold values from 0 to 15
Outputs:
- band_gradient: float32 [2048, 1152], P(('chain', 'aux'))
- polarization: float32 [32, 32], P('aux')
All inputs are finite; a program needn't handle non-finite values.
Results may differ from a plain program's by a relative error of at most 0.0042.
Values may be sent and summed in bfloat16 or wider, within the bound.
No kernel may reach another device: no remote copies, remote signals or barrier semaphores. Data moves between devices by JAX's collectives and lax.ppermute only.
A program may use at most 128 MiB of HBM per device.

v0:
```python
import math
import jax
import jax.numpy as jnp
from jax import lax
from jax.sharding import PartitionSpec as P


def passed_along(block, axis, distance):
    devices = range(lax.axis_size(axis))
    route = [(i - distance, i) for i in devices if i - distance in devices]
    return lax.ppermute(block, axis, route)


def shift_blocks(matrix, offset, block_size):
    if offset == 0:
        return matrix
    padding = jnp.zeros(matrix.shape[:-1] + (abs(offset) * block_size,), matrix.dtype)
    if offset > 0:
        return jnp.concatenate([padding, matrix[..., : -offset * block_size]], -1)
    return jnp.concatenate([matrix[..., -offset * block_size :], padding], -1)


def body(occupied, virtual, three_centre, kernel, profile, atom_map):
    block_size = occupied.shape[0]
    band_cols = occupied.shape[1]
    slots_total = band_cols // block_size
    spread = (slots_total - 1) // 2
    nblocks = lax.axis_size("chain")
    position = lax.axis_index("chain")
    slot_ids = jnp.arange(slots_total, dtype=jnp.int32)
    block_ids = jnp.arange(nblocks, dtype=jnp.int32)
    others = position + slot_ids - spread
    neighbours = jnp.sum(jnp.where(block_ids[None, :] == others[:, None], profile[None, :], 0), 1)
    own_width = jnp.sum(jnp.where(block_ids == position, profile, 0))
    allowed = jnp.abs(slot_ids - spread) <= jnp.minimum(own_width, neighbours)
    column_keep = jnp.repeat(allowed, block_size)
    zero_half = jnp.zeros((), jnp.bfloat16)
    occ_masked = jnp.where(column_keep[None, :], occupied, zero_half)
    vir_masked = jnp.where(column_keep[None, :], virtual, zero_half)
    both_bands = jnp.stack([occ_masked, vir_masked])
    fetched = []
    for slot_index in range(slots_total):
        if slot_index == spread:
            fetched.append(both_bands)
        else:
            fetched.append(passed_along(both_bands, "chain", spread - slot_index))
    stack_occ = jnp.concatenate(
        [shift_blocks(fetched[k][0], k - spread, block_size) for k in range(slots_total)], 0
    )
    stack_vir = jnp.concatenate(
        [shift_blocks(fetched[k][1], k - spread, block_size) for k in range(slots_total)], 0
    )
    aux_here = three_centre.shape[0]
    aux_total = kernel.shape[1]
    screen = jnp.abs(atom_map - position) <= nblocks // 4
    local = jnp.where(column_keep[None, None, :] & screen[:, None, None], three_centre, zero_half)
    screened = local.reshape(aux_here * block_size, band_cols)
    coupled = jnp.dot(screened, stack_occ, preferred_element_type=jnp.float32).astype(jnp.bfloat16)
    coupled = coupled.reshape(aux_here, block_size * band_cols)
    partner = jnp.dot(screened, stack_vir, preferred_element_type=jnp.float32).astype(jnp.bfloat16)
    partner = partner.reshape(aux_here, block_size, band_cols)
    piece = lax.all_gather(partner, "aux", axis=0, tiled=True)
    piece_rows = piece.shape[0]
    columns = piece.reshape(piece_rows, block_size * band_cols)
    products = lax.dot_general(
        coupled, columns, (((1,), (1,)), ((), ())), preferred_element_type=jnp.float32
    )
    polar_part = products
    response_sum = jnp.dot(kernel, columns, preferred_element_type=jnp.float32)
    polar_part, response_sum = (polar_part, response_sum)
    polarization = lax.psum(polar_part, "chain") * (
        1.0 / math.sqrt(block_size * nblocks * band_cols)
    )
    response = response_sum.astype(jnp.bfloat16).reshape(aux_here * block_size, band_cols)
    partials = lax.dot_general(
        screened, response, (((0,), (0,)), ((), ())), preferred_element_type=jnp.float32
    )
    partials = partials.reshape(slots_total, block_size, band_cols)
    gathered_sum = partials[spread]
    for slot_index in range(slots_total):
        if slot_index != spread:
            moved = shift_blocks(partials[slot_index], spread - slot_index, block_size)
            gathered_sum = gathered_sum + passed_along(moved, "chain", slot_index - spread)
    gathered_sum = lax.psum_scatter(gathered_sum, "aux", scatter_dimension=0, tiled=True)
    scale_grad = 1.0 / math.sqrt(block_size * aux_total)
    band_gradient = (
        jnp.where(column_keep[None, :], gathered_sum, jnp.zeros((), jnp.float32)) * scale_grad
    )
    return (band_gradient, polarization)


def solution(mesh):
    placed = (
        P("chain", None),
        P("chain", None),
        P("aux", "chain", None),
        P("aux", None),
        P(),
        P("aux"),
    )
    return jax.shard_map(
        body,
        mesh=mesh,
        in_specs=placed,
        out_specs=(P(("chain", "aux"), None), P("aux", None)),
        check_vma=False,
    )
```

profile of v0, /device:TPU:0, one launch (start us, length us, event | category | flops | bytes accessed | tf_op | source)
XLA Modules:
  0.0 369.4 jit_solution(13112788531242796778)
XLA Ops:
  7.2 1.3 fusion.12
  8.5 0.8 select_reduce_fusion
  9.4 0.7 minimum_compare_fusion
  10.1 1.1 fusion.9
  11.3 1.3 collective-permute-start.7
  12.6 1.3 collective-permute-start.6
  13.9 1.3 collective-permute-start.5
  15.2 1.3 collective-permute-start.4
  16.5 3.1 collective-permute-start.3
  19.6 0.7 abs_compare_fusion
  20.2 0.1 broadcast_and_fusion
  20.3 2.8 broadcast_select_fusion
  23.2 7.3 %collective-permute-done.7 = bf16[2,128,1152]{2,1,0:T(8,128)(2,1)S(1)} collective-permute-done((bf16[2,128,1152]{2,1,0:T(8,128)(2,1)S(1)}, bf16[2,128,1152]{2,1,0:T(8,128)(2,1)S(1)}, u32[]{:S(2)}, u32[]{:S(2)}) %collective-permute-start.7) | collective-permute-done | bytes 589856 | tf_op jit(solution)/shard_map/ppermute | solution.py:11
  30.4 2.8 collective-permute-start.2
  33.3 6.0 %collective-permute-start.1 = (bf16[2,128,1152]{2,1,0:T(8,128)(2,1)S(1)}, bf16[2,128,1152]{2,1,0:T(8,128)(2,1)S(1)}, u32[]{:S(2)}, u32[]{:S(2)}) collective-permute-start(bf16[2,128,1152]{2,1,0:T(8,128)(2,1)S(1)} %pad_maximum_fusion), channel_id=1, source_target_pairs={{0,6},{2,8},{4,10},{6,12},{8,14},{10,16},{12,18},{14,20},{16,22},{... | collective-permute-start | bytes 1769480 | tf_op jit(solution)/shard_map/ppermute | solution.py:11
  39.3 24.2 %collective-permute-start = (bf16[2,128,1152]{2,1,0:T(8,128)(2,1)S(1)}, bf16[2,128,1152]{2,1,0:T(8,128)(2,1)S(1)}, u32[]{:S(2)}, u32[]{:S(2)}) collective-permute-start(bf16[2,128,1152]{2,1,0:T(8,128)(2,1)S(1)} %pad_maximum_fusion), channel_id=1, source_target_pairs={{0,8},{2,10},{4,12},{6,14},{8,16},{10,18},{12,20},{14,22},{16,24},... | collective-permute-start | bytes 1769480 | tf_op jit(solution)/shard_map/ppermute | solution.py:11
  63.7 4.2 %collective-permute-done.2 = bf16[2,128,1152]{2,1,0:T(8,128)(2,1)S(1)} collective-permute-done((bf16[2,128,1152]{2,1,0:T(8,128)(2,1)S(1)}, bf16[2,128,1152]{2,1,0:T(8,128)(2,1)S(1)}, u32[]{:S(2)}, u32[]{:S(2)}) %collective-permute-start.2) | collective-permute-done | bytes 589856 | tf_op jit(solution)/shard_map/ppermute | solution.py:11
  68.2 6.0 %collective-permute-done.1 = bf16[2,128,1152]{2,1,0:T(8,128)(2,1)S(1)} collective-permute-done((bf16[2,128,1152]{2,1,0:T(8,128)(2,1)S(1)}, bf16[2,128,1152]{2,1,0:T(8,128)(2,1)S(1)}, u32[]{:S(2)}, u32[]{:S(2)}) %collective-permute-start.1) | collective-permute-done | bytes 589856 | tf_op jit(solution)/shard_map/ppermute | solution.py:11
  74.7 0.6 copy-done.3
  75.3 0.1 copy-done.4
  75.4 0.1 fusion.8
  75.6 0.1 pad_dynamic-update-slice_fusion.3
  75.8 8.6 %convolution_convert_fusion.2 = bf16[2048,1152]{1,0:T(8,128)(2,1)} fusion(bf16[2048,1152]{1,0:T(8,128)(2,1)S(1)} %bitcast.58, bf16[1152,1152]{1,0:T(8,128)(2,1)S(1)} %pad_dynamic-update-slice_fusion.8), kind=kOutput, calls=%fused_computation.3 | convolution fusion | flops 5438177280 | bytes 12091392 | tf_op jit(solution)/shard_map/dot_general | solution.py:60
  84.4 0.2 reduce-scatter.2.cloned.1.call-start
  84.7 122.4 %all-gather.2.cloned.1.call-done = bf16[32,128,1152]{2,1,0:T(8,128)(2,1)} async-done(((bf16[16,128,1152]{2,1,0:T(8,128)(2,1)}), bf16[32,128,1152]{2,1,0:T(8,128)(2,1)}) %all-gather.2.cloned.1.call-update) | async-done | bytes 9437200 | tf_op jit(solution)/shard_map/all_gather | solution.py:62
  207.0 12.8 %copy.8 = bf16[4,8,128,1152]{3,1,2,0:T(8,128)(2,1)} copy(bf16[4,8,128,1152]{3,2,1,0:T(8,128)(2,1)} %bitcast.56) | data formatting | bytes 18874368
  219.8 7.2 %fusion = bf16[16,147456]{1,0:T(8,128)(2,1)} fusion(bf16[16,32]{1,0:T(8,128)(2,1)S(1)} %copy-done, bf16[32,147456]{1,0:T(8,128)(2,1)} %bitcast.54), kind=kOutput, calls=%fused_computation.1 | convolution fusion | flops 153354240 | bytes 14156800 | tf_op jit(solution)/shard_map/dot_general | solution.py:69
  227.0 5.3 %reshape.79 = bf16[2048,1152]{1,0:T(8,128)(2,1)} reshape(bf16[16,147456]{1,0:T(8,128)(2,1)} %fusion) | data formatting | bytes 9437184 | tf_op jit(solution)/shard_map/reshape | solution.py:74
  232.2 10.3 %fusion.17 = f32[1152,1152]{1,0:T(8,128)S(1)} fusion(bf16[2048,1152]{1,0:T(8,128)(2,1)} %bitcast.59, bf16[2048,1152]{1,0:T(8,128)(2,1)} %reshape.79), kind=kOutput, calls=%fused_computation.67 | convolution fusion | flops 5435817984 | bytes 14745600 | tf_op jit(solution)/shard_map/dot_general | solution.py:75
  242.8 3.4 collective-permute-start.15
  246.2 1.3 collective-permute-start.8
  247.6 2.4 collective-permute-start.14
  250.0 1.3 collective-permute-start.9
  251.5 4.3 %collective-permute-start.13 = (f32[128,1152]{1,0:T(8,128)S(1)}, f32[128,1152]{1,0:T(8,128)S(1)}, u32[]{:S(2)}, u32[]{:S(2)}) collective-permute-start(f32[128,1152]{1,0:T(8,128)S(1)} %concatenate.92), channel_id=1, source_target_pairs={{0,4},{2,6},{4,8},{6,10},{8,12},{10,14},{12,16},{14,18},{16,20},{1... | collective-permute-start | bytes 1769480 | tf_op jit(solution)/shard_map/ppermute | solution.py:11
  255.8 0.1 fusion.16
  256.0 3.8 %collective-permute-done.15 = f32[128,1152]{1,0:T(8,128)S(1)} collective-permute-done((f32[128,1152]{1,0:T(8,128)S(1)}, f32[128,1152]{1,0:T(8,128)S(1)}, u32[]{:S(2)}, u32[]{:S(2)}) %collective-permute-start.15) | collective-permute-done | bytes 589856 | tf_op jit(solution)/shard_map/ppermute | solution.py:11
  259.9 1.3 collective-permute-start.10
  261.2 3.1 collective-permute-done.8
  264.3 1.3 collective-permute-start.12
  265.6 1.3 collective-permute-start.11
  267.1 27.6 %collective-permute-done.13 = f32[128,1152]{1,0:T(8,128)S(1)} collective-permute-done((f32[128,1152]{1,0:T(8,128)S(1)}, f32[128,1152]{1,0:T(8,128)S(1)}, u32[]{:S(2)}, u32[]{:S(2)}) %collective-permute-start.13) | collective-permute-done | bytes 589856 | tf_op jit(solution)/shard_map/ppermute | solution.py:11
  294.7 1.1 fusion.7
  295.8 10.4 %convolution_convert_fusion.1 = bf16[2048,1152]{1,0:T(8,128)(2,1)} fusion(bf16[2048,1152]{1,0:T(8,128)(2,1)} %bitcast.60, bf16[1152,1152]{1,0:T(8,128)(2,1)S(1)} %pad_dynamic-update-slice_fusion), kind=kOutput, calls=%fused_computation.2 | convolution fusion | flops 5438177280 | bytes 12091392 | tf_op jit(solution)/shard_map/dot_general | solution.py:58
  306.2 5.3 %reshape.80 = bf16[16,147456]{1,0:T(8,128)(2,1)} reshape(bf16[2048,1152]{1,0:T(8,128)(2,1)} %convolution_convert_fusion.1) | data formatting | bytes 9437184 | tf_op jit(solution)/shard_map/reshape | solution.py:59
  311.5 7.8 %fusion.18 = f32[16,32]{1,0:T(8,128)S(1)} fusion(bf16[16,147456]{1,0:T(8,128)(2,1)} %reshape.80, bf16[32,147456]{1,0:T(8,128)(2,1)} %bitcast.55), kind=kOutput, calls=%fused_computation.68 | convolution fusion | flops 150994944 | bytes 14157824 | tf_op jit(solution)/shard_map/dot_general | solution.py:65
  319.3 40.9 %psum.7 = f32[16,32]{1,0:T(8,128)S(1)} all-reduce(f32[16,32]{1,0:T(8,128)S(1)} %fusion.18), channel_id=1, replica_groups=mesh['chain'=16,'aux'=2] {'chain'}, use_global_device_ids=true, to_apply=%region_3.4 | all-reduce | flops 512 | bytes 4096 | tf_op jit(solution)/shard_map/psum | solution.py:71
  360.3 0.6 broadcast_multiply_fusion
  360.9 1.7 select_multiply_fusion
  (74 shorter events, 1.8 us)
Async XLA Ops:
  7.2 212.6 %copy-start = (bf16[16,32]{1,0:T(8,128)(2,1)S(1)}, bf16[16,32]{1,0:T(8,128)(2,1)}, u32[]{:S(2)}) copy-start(bf16[16,32]{1,0:T(8,128)(2,1)} %param.9) | copy-start | bytes 3076
  7.2 199.8 %all-gather.2.cloned.1.call-start = ((), (), s32[]{:S(2)}) async-start(), calls=%async_computation.1 | async-start | bytes 14155776 | tf_op jit(solution)/shard_map/all_gather | solution.py:62
  11.3 19.1 %collective-permute-start.7 = (bf16[2,128,1152]{2,1,0:T(8,128)(2,1)S(1)}, bf16[2,128,1152]{2,1,0:T(8,128)(2,1)S(1)}, u32[]{:S(2)}, u32[]{:S(2)}) collective-permute-start(bf16[2,128,1152]{2,1,0:T(8,128)(2,1)S(1)} %pad_maximum_fusion), channel_id=1, source_target_pairs={{8,0},{10,2},{12,4},{14,6},{16,8},{18,10},{20,12},{22,14},{24,16},... | collective-permute-start | bytes 1769480 | tf_op jit(solution)/shard_map/ppermute | solution.py:11
  12.6 20.7 %collective-permute-start.6 = (bf16[2,128,1152]{2,1,0:T(8,128)(2,1)S(1)}, bf16[2,128,1152]{2,1,0:T(8,128)(2,1)S(1)}, u32[]{:S(2)}, u32[]{:S(2)}) collective-permute-start(bf16[2,128,1152]{2,1,0:T(8,128)(2,1)S(1)} %pad_maximum_fusion), channel_id=1, source_target_pairs={{6,0},{8,2},{10,4},{12,6},{14,8},{16,10},{18,12},{20,14},{22,16},{... | collective-permute-start | bytes 1769480 | tf_op jit(solution)/shard_map/ppermute | solution.py:11
  13.9 25.4 %collective-permute-start.5 = (bf16[2,128,1152]{2,1,0:T(8,128)(2,1)S(1)}, bf16[2,128,1152]{2,1,0:T(8,128)(2,1)S(1)}, u32[]{:S(2)}, u32[]{:S(2)}) collective-permute-start(bf16[2,128,1152]{2,1,0:T(8,128)(2,1)S(1)} %pad_maximum_fusion), channel_id=1, source_target_pairs={{4,0},{6,2},{8,4},{10,6},{12,8},{14,10},{16,12},{18,14},{20,16},{2... | collective-permute-start | bytes 1769480 | tf_op jit(solution)/shard_map/ppermute | solution.py:11
  15.2 48.4 %collective-permute-start.4 = (bf16[2,128,1152]{2,1,0:T(8,128)(2,1)S(1)}, bf16[2,128,1152]{2,1,0:T(8,128)(2,1)S(1)}, u32[]{:S(2)}, u32[]{:S(2)}) collective-permute-start(bf16[2,128,1152]{2,1,0:T(8,128)(2,1)S(1)} %pad_maximum_fusion), channel_id=1, source_target_pairs={{2,0},{4,2},{6,4},{8,6},{10,8},{12,10},{14,12},{16,14},{18,16},{20... | collective-permute-start | bytes 1769480 | tf_op jit(solution)/shard_map/ppermute | solution.py:11
  16.5 47.1 %collective-permute-start.3 = (bf16[2,128,1152]{2,1,0:T(8,128)(2,1)S(1)}, bf16[2,128,1152]{2,1,0:T(8,128)(2,1)S(1)}, u32[]{:S(2)}, u32[]{:S(2)}) collective-permute-start(bf16[2,128,1152]{2,1,0:T(8,128)(2,1)S(1)} %pad_maximum_fusion), channel_id=1, source_target_pairs={{0,2},{2,4},{4,6},{6,8},{8,10},{10,12},{12,14},{14,16},{16,18},{18... | collective-permute-start | bytes 1769480 | tf_op jit(solution)/shard_map/ppermute | solution.py:11
  23.1 52.6 %copy-start.2 = (bf16[16,128,1152]{2,1,0:T(8,128)(2,1)}, bf16[16,128,1152]{2,1,0:T(8,128)(2,1)S(1)}, u32[]{:S(2)}) copy-start(bf16[16,128,1152]{2,1,0:T(8,128)(2,1)S(1)} %broadcast_select_fusion) | copy-start | bytes 14155780
  30.4 37.5 %collective-permute-start.2 = (bf16[2,128,1152]{2,1,0:T(8,128)(2,1)S(1)}, bf16[2,128,1152]{2,1,0:T(8,128)(2,1)S(1)}, u32[]{:S(2)}, u32[]{:S(2)}) collective-permute-start(bf16[2,128,1152]{2,1,0:T(8,128)(2,1)S(1)} %pad_maximum_fusion), channel_id=1, source_target_pairs={{0,4},{2,6},{4,8},{6,10},{8,12},{10,14},{12,16},{14,18},{16,20},{1... | collective-permute-start | bytes 1769480 | tf_op jit(solution)/shard_map/ppermute | solution.py:11
  33.3 41.0 %collective-permute-start.1 = (bf16[2,128,1152]{2,1,0:T(8,128)(2,1)S(1)}, bf16[2,128,1152]{2,1,0:T(8,128)(2,1)S(1)}, u32[]{:S(2)}, u32[]{:S(2)}) collective-permute-start(bf16[2,128,1152]{2,1,0:T(8,128)(2,1)S(1)} %pad_maximum_fusion), channel_id=1, source_target_pairs={{0,6},{2,8},{4,10},{6,12},{8,14},{10,16},{12,18},{14,20},{16,22},{... | collective-permute-start | bytes 1769480 | tf_op jit(solution)/shard_map/ppermute | solution.py:11
  39.3 35.0 %collective-permute-start = (bf16[2,128,1152]{2,1,0:T(8,128)(2,1)S(1)}, bf16[2,128,1152]{2,1,0:T(8,128)(2,1)S(1)}, u32[]{:S(2)}, u32[]{:S(2)}) collective-permute-start(bf16[2,128,1152]{2,1,0:T(8,128)(2,1)S(1)} %pad_maximum_fusion), channel_id=1, source_target_pairs={{0,8},{2,10},{4,12},{6,14},{8,16},{10,18},{12,20},{14,22},{16,24},... | collective-permute-start | bytes 1769480 | tf_op jit(solution)/shard_map/ppermute | solution.py:11
  74.4 1.0 copy-start.3
  74.4 1.0 copy-start.4
  84.4 276.4 %reduce-scatter.2.cloned.1.call-start = ((), (), s32[]{:S(2)}) async-start(), calls=%async_computation.2 | async-start | bytes 884736 | tf_op jit(solution)/shard_map/reduce_scatter | solution.py:84
  242.8 17.1 %collective-permute-start.15 = (f32[128,1152]{1,0:T(8,128)S(1)}, f32[128,1152]{1,0:T(8,128)S(1)}, u32[]{:S(2)}, u32[]{:S(2)}) collective-permute-start(f32[128,1152]{1,0:T(8,128)S(1)} %concatenate.94), channel_id=1, source_target_pairs={{0,8},{2,10},{4,12},{6,14},{8,16},{10,18},{12,20},{14,22},{16,24},... | collective-permute-start | bytes 1769480 | tf_op jit(solution)/shard_map/ppermute | solution.py:11
  246.2 18.1 %collective-permute-start.8 = (f32[128,1152]{1,0:T(8,128)S(1)}, f32[128,1152]{1,0:T(8,128)S(1)}, u32[]{:S(2)}, u32[]{:S(2)}) collective-permute-start(f32[128,1152]{1,0:T(8,128)S(1)} %concatenate.87), channel_id=1, source_target_pairs={{8,0},{10,2},{12,4},{14,6},{16,8},{18,10},{20,12},{22,14},{24,16},... | collective-permute-start | bytes 1769480 | tf_op jit(solution)/shard_map/ppermute | solution.py:11
  247.6 18.1 %collective-permute-start.14 = (f32[128,1152]{1,0:T(8,128)S(1)}, f32[128,1152]{1,0:T(8,128)S(1)}, u32[]{:S(2)}, u32[]{:S(2)}) collective-permute-start(f32[128,1152]{1,0:T(8,128)S(1)} %concatenate.93), channel_id=1, source_target_pairs={{0,6},{2,8},{4,10},{6,12},{8,14},{10,16},{12,18},{14,20},{16,22},{... | collective-permute-start | bytes 1769480 | tf_op jit(solution)/shard_map/ppermute | solution.py:11
  250.0 17.0 %collective-permute-start.9 = (f32[128,1152]{1,0:T(8,128)S(1)}, f32[128,1152]{1,0:T(8,128)S(1)}, u32[]{:S(2)}, u32[]{:S(2)}) collective-permute-start(f32[128,1152]{1,0:T(8,128)S(1)} %concatenate.88), channel_id=1, source_target_pairs={{6,0},{8,2},{10,4},{12,6},{14,8},{16,10},{18,12},{20,14},{22,16},{... | collective-permute-start | bytes 1769480 | tf_op jit(solution)/shard_map/ppermute | solution.py:11
  251.5 43.2 %collective-permute-start.13 = (f32[128,1152]{1,0:T(8,128)S(1)}, f32[128,1152]{1,0:T(8,128)S(1)}, u32[]{:S(2)}, u32[]{:S(2)}) collective-permute-start(f32[128,1152]{1,0:T(8,128)S(1)} %concatenate.92), channel_id=1, source_target_pairs={{0,4},{2,6},{4,8},{6,10},{8,12},{10,14},{12,16},{14,18},{16,20},{1... | collective-permute-start | bytes 1769480 | tf_op jit(solution)/shard_map/ppermute | solution.py:11
  259.9 34.8 %collective-permute-start.10 = (f32[128,1152]{1,0:T(8,128)S(1)}, f32[128,1152]{1,0:T(8,128)S(1)}, u32[]{:S(2)}, u32[]{:S(2)}) collective-permute-start(f32[128,1152]{1,0:T(8,128)S(1)} %concatenate.89), channel_id=1, source_target_pairs={{4,0},{6,2},{8,4},{10,6},{12,8},{14,10},{16,12},{18,14},{20,16},{2... | collective-permute-start | bytes 1769480 | tf_op jit(solution)/shard_map/ppermute | solution.py:11
  264.3 30.4 %collective-permute-start.12 = (f32[128,1152]{1,0:T(8,128)S(1)}, f32[128,1152]{1,0:T(8,128)S(1)}, u32[]{:S(2)}, u32[]{:S(2)}) collective-permute-start(f32[128,1152]{1,0:T(8,128)S(1)} %concatenate.91), channel_id=1, source_target_pairs={{0,2},{2,4},{4,6},{6,8},{8,10},{10,12},{12,14},{14,16},{16,18},{18... | collective-permute-start | bytes 1769480 | tf_op jit(solution)/shard_map/ppermute | solution.py:11
  265.6 29.0 %collective-permute-start.11 = (f32[128,1152]{1,0:T(8,128)S(1)}, f32[128,1152]{1,0:T(8,128)S(1)}, u32[]{:S(2)}, u32[]{:S(2)}) collective-permute-start(f32[128,1152]{1,0:T(8,128)S(1)} %concatenate.90), channel_id=1, source_target_pairs={{2,0},{4,2},{6,4},{8,6},{10,8},{12,10},{14,12},{16,14},{18,16},{20... | collective-permute-start | bytes 1769480 | tf_op jit(solution)/shard_map/ppermute | solution.py:11
  311.5 51.1 %copy-start.1 = (bf16[16,32]{1,0:T(8,128)(2,1)S(1)}, bf16[16,32]{1,0:T(8,128)(2,1)}, u32[]{:S(2)}) copy-start(bf16[16,32]{1,0:T(8,128)(2,1)} %param.9) | copy-start | bytes 3076
Sparse Core Ops, SparseCore 0:
  84.5 122.4 all-gather.1
  295.9 25.7 reduce-scatter.1
where the time goes:
time: 370 us; the launch traced here: 369 us
  waiting for transfers between devices  174 us (47%)
  starting transfers between devices  58 us (16%)
  matrix products  44.4 us (12%)
  blocking collectives  40.9 us (11%)
  local copies, waits for them, and re-layouts  25.8 us (7%)
  between operations  14.7 us (4%)
  other arithmetic  11.1 us (3%)
    all_gather x1, waiting for transfers between devices, body(): piece = lax.all_gather(partner, 'aux', axis=0, tiled=True)  122 us
    ppermute x16, starting transfers between devices, passed_along(): return lax.ppermute(block, axis, route)  57.8 us
    ppermute x16, waiting for transfers between devices, passed_along(): return lax.ppermute(block, axis, route)  52.1 us
    psum x1, blocking collectives, body(): lax.psum(polar_part, 'chain')  40.9 us
    unnamed x24, local copies, waits for them, and re-layouts  13.9 us
    dot_general x1, matrix products, body(): jnp.dot(screened, stack_occ, preferred_element_type=jnp.float32)  10.4 us
    dot_general x1, matrix products, body(): lax.dot_general(screened, response, (((0,), (0,)), ((), ())), preferred_e...  10.3 us
    dot_general x1, matrix products, body(): jnp.dot(screened, stack_vir, preferred_element_type=jnp.float32)  8.63 us
  transfers between devices with their start and end apart: 18, of which 7 were waited for; matrix products, arithmetic and copies ran while one was open for 8% of the time, Pallas kernels for 0%

commit v1 on v0

--- a/solution.py
+++ b/solution.py
@@ -59,7 +59,10 @@
     coupled = coupled.reshape(aux_here, block_size * band_cols)
     partner = jnp.dot(screened, stack_vir, preferred_element_type=jnp.float32).astype(jnp.bfloat16)
     partner = partner.reshape(aux_here, block_size, band_cols)
-    piece = lax.all_gather(partner, "aux", axis=0, tiled=True)
+    size = lax.axis_size("aux")
+    blocks = jnp.stack([partner for _ in range(size)])
+    blocks = lax.all_to_all(blocks, "aux", split_axis=0, concat_axis=0)
+    piece = jnp.concatenate(blocks, axis=0)
     piece_rows = piece.shape[0]
     columns = piece.reshape(piece_rows, block_size * band_cols)
     products = lax.dot_general(

time: 370 us -> 377 us (1.019)
  blocking collectives: 40.9 us -> 139 us
  waiting for transfers between devices: 174 us -> 84.5 us
  starting transfers between devices: 58 us -> 48.5 us
  other arithmetic: 11.1 us -> 19.5 us
    all_gather x1 -> x0, waiting for transfers between devices: 122 us -> none  [body(): piece = lax.all_gather(partner, 'aux', axis=0, tiled=True)]
    all_to_all x0 -> x1, blocking collectives: none -> 109 us  [body(): blocks = lax.all_to_all(blocks, 'aux', split_axis=0, concat_axis=0)]
    ppermute x16, waiting for transfers between devices: 52.1 us -> 84.5 us  [passed_along(): return lax.ppermute(block, axis, route)]
    psum x1, blocking collectives: 40.9 us -> 30 us  [body(): lax.psum(polar_part, 'chain')]
    ppermute x16, starting transfers between devices: 57.8 us -> 48.5 us  [passed_along(): return lax.ppermute(block, axis, route)]
    another operation x0 -> x1, other arithmetic: none -> 8.35 us  [body(): blocks = jnp.stack([partner for _ in range(size)])]
  transfers between devices with their start and end apart: 18 -> 17, of which waited for: 7 -> 6; matrix products, arithmetic and copies ran while one was open for 8% -> 8% of each run, Pallas kernels for 0% -> 0%
where the time goes in v1:
time: 377 us; the launch traced here: 376 us
  blocking collectives  139 us (37%)
  waiting for transfers between devices  84.5 us (22%)
  starting transfers between devices  48.5 us (13%)
  matrix products  44.2 us (12%)
  local copies, waits for them, and re-layouts  25.1 us (7%)
  other arithmetic  19.5 us (5%)
  between operations  14.7 us (4%)
    all_to_all x1, blocking collectives, body(): blocks = lax.all_to_all(blocks, 'aux', split_axis=0, concat_axis=0)  109 us
    ppermute x16, waiting for transfers between devices, passed_along(): return lax.ppermute(block, axis, route)  84.5 us
    ppermute x16, starting transfers between devices, passed_along(): return lax.ppermute(block, axis, route)  48.5 us
    psum x1, blocking collectives, body(): lax.psum(polar_part, 'chain')  30 us
    unnamed x24, local copies, waits for them, and re-layouts  13.2 us
    dot_general x1, matrix products, body(): jnp.dot(screened, stack_occ, preferred_element_type=jnp.float32)  10.4 us
    dot_general x1, matrix products, body(): lax.dot_general(screened, response, (((0,), (0,)), ((), ())), preferred_e...  10.3 us
    dot_general x1, matrix products, body(): jnp.dot(screened, stack_vir, preferred_element_type=jnp.float32)  8.56 us
  transfers between devices with their start and end apart: 17, of which 6 were waited for; matrix products, arithmetic and copies ran while one was open for 8% of the time, Pallas kernels for 0%

profile of v1, /device:TPU:0, one launch (start us, length us, event | category | flops | bytes accessed | tf_op | source)
XLA Modules:
  0.0 375.5 jit_solution(5415388500980510361)
XLA Ops:
  7.2 1.3 fusion.12
  8.5 0.8 select_reduce_fusion
  9.4 0.7 minimum_compare_fusion
  10.0 0.1 broadcast_bitcast_fusion
  10.1 1.1 fusion.9
  11.2 0.1 pad_maximum_fusion.1
  11.3 5.0 %collective-permute-start = (bf16[2,128,1152]{2,1,0:T(8,128)(2,1)S(1)}, bf16[2,128,1152]{2,1,0:T(8,128)(2,1)S(1)}, u32[]{:S(2)}, u32[]{:S(2)}) collective-permute-start(bf16[2,128,1152]{2,1,0:T(8,128)(2,1)S(1)} %pad_maximum_fusion.1), channel_id=1, source_target_pairs={{0,8},{2,10},{4,12},{6,14},{8,16},{10,18},{12,20},{14,22},{16,24},... | collective-permute-start | bytes 1769480 | tf_op jit(solution)/shard_map/ppermute | solution.py:11
  16.3 2.6 collective-permute-start.1
  18.9 3.4 collective-permute-start.2
  22.4 2.6 collective-permute-start.3
  25.0 1.3 collective-permute-start.4
  26.3 0.7 abs_compare_fusion
  27.0 0.1 broadcast_and_fusion
  27.1 2.8 broadcast_select_fusion
  30.0 1.3 collective-permute-start.5
  31.3 1.3 collective-permute-start.6
  32.7 34.4 %collective-permute-done.2 = bf16[2,128,1152]{2,1,0:T(8,128)(2,1)S(1)} collective-permute-done((bf16[2,128,1152]{2,1,0:T(8,128)(2,1)S(1)}, bf16[2,128,1152]{2,1,0:T(8,128)(2,1)S(1)}, u32[]{:S(2)}, u32[]{:S(2)}) %collective-permute-start.2) | collective-permute-done | bytes 589856 | tf_op jit(solution)/shard_map/ppermute | solution.py:11
  67.1 1.3 collective-permute-start.7
  69.1 9.8 %collective-permute-done.7 = bf16[2,128,1152]{2,1,0:T(8,128)(2,1)S(1)} collective-permute-done((bf16[2,128,1152]{2,1,0:T(8,128)(2,1)S(1)}, bf16[2,128,1152]{2,1,0:T(8,128)(2,1)S(1)}, u32[]{:S(2)}, u32[]{:S(2)}) %collective-permute-start.7) | collective-permute-done | bytes 589856 | tf_op jit(solution)/shard_map/ppermute | solution.py:11
  79.1 0.1 fusion.8
  79.3 0.1 pad_dynamic-update-slice_fusion.3
  79.5 8.6 %convolution_convert_fusion.2 = bf16[2048,1152]{1,0:T(8,128)(2,1)} fusion(bf16[2048,1152]{1,0:T(8,128)(2,1)S(1)} %bitcast.59, bf16[1152,1152]{1,0:T(8,128)(2,1)S(1)} %pad_dynamic-update-slice_fusion.8), kind=kOutput, calls=%fused_computation.4 | convolution fusion | flops 5438177280 | bytes 12091392 | tf_op jit(solution)/shard_map/dot_general | solution.py:60
  88.0 8.4 %pad_maximum_fusion = bf16[2,16,128,1152]{3,2,1,0:T(8,128)(2,1)} fusion(bf16[1,16,128,1152]{3,2,1,0:T(8,128)(2,1)} %bitcast.58), kind=kLoop, calls=%fused_computation.2 | loop fusion | flops 4718592 | bytes 14155776 | tf_op jit(solution)/shard_map/stack | solution.py:63
  96.4 109.1 %all_to_all.5 = bf16[2,16,128,1152]{3,2,1,0:T(8,128)(2,1)} all-to-all(bf16[2,16,128,1152]{3,2,1,0:T(8,128)(2,1)} %pad_maximum_fusion), channel_id=1, replica_groups=mesh['chain'=16,'aux'=2] {'aux'}, dimensions={0} | all-to-all | bytes 18874368 | tf_op jit(solution)/shard_map/all_to_all | solution.py:64
  205.5 12.8 %copy.8 = bf16[4,8,128,1152]{3,1,2,0:T(8,128)(2,1)} copy(bf16[4,8,128,1152]{3,2,1,0:T(8,128)(2,1)} %bitcast.57) | data formatting | bytes 18874368
  218.2 7.2 %fusion = bf16[16,147456]{1,0:T(8,128)(2,1)} fusion(bf16[16,32]{1,0:T(8,128)(2,1)S(1)} %copy-done, bf16[32,147456]{1,0:T(8,128)(2,1)} %bitcast.55), kind=kOutput, calls=%fused_computation.1 | convolution fusion | flops 153354240 | bytes 14156800 | tf_op jit(solution)/shard_map/dot_general | solution.py:72
  225.4 5.2 %reshape.71 = bf16[2048,1152]{1,0:T(8,128)(2,1)} reshape(bf16[16,147456]{1,0:T(8,128)(2,1)} %fusion) | data formatting | bytes 9437184 | tf_op jit(solution)/shard_map/reshape | solution.py:77
  230.6 10.3 %fusion.17 = f32[1152,1152]{1,0:T(8,128)S(1)} fusion(bf16[2048,1152]{1,0:T(8,128)(2,1)} %bitcast.60, bf16[2048,1152]{1,0:T(8,128)(2,1)} %reshape.71), kind=kOutput, calls=%fused_computation.68 | convolution fusion | flops 5435817984 | bytes 14745600 | tf_op jit(solution)/shard_map/dot_general | solution.py:78
  240.9 0.1 fusion.16
  241.1 0.1 fusion.15
  241.2 1.3 collective-permute-start.11
  242.5 3.1 collective-permute-start.12
  245.7 1.3 collective-permute-start.10
  247.0 5.1 %collective-permute-start.13 = (f32[128,1152]{1,0:T(8,128)S(1)}, f32[128,1152]{1,0:T(8,128)S(1)}, u32[]{:S(2)}, u32[]{:S(2)}) collective-permute-start(f32[128,1152]{1,0:T(8,128)S(1)} %concatenate.92), channel_id=1, source_target_pairs={{0,4},{2,6},{4,8},{6,10},{8,12},{10,14},{12,16},{14,18},{16,20},{1... | collective-permute-start | bytes 1769480 | tf_op jit(solution)/shard_map/ppermute | solution.py:11
  252.3 11.6 %collective-permute-start.14 = (f32[128,1152]{1,0:T(8,128)S(1)}, f32[128,1152]{1,0:T(8,128)S(1)}, u32[]{:S(2)}, u32[]{:S(2)}) collective-permute-start(f32[128,1152]{1,0:T(8,128)S(1)} %concatenate.93), channel_id=1, source_target_pairs={{0,6},{2,8},{4,10},{6,12},{8,14},{10,16},{12,18},{14,20},{16,22},{... | collective-permute-start | bytes 1769480 | tf_op jit(solution)/shard_map/ppermute | solution.py:11
  264.1 1.3 collective-permute-start.9
  265.4 4.7 %collective-permute-start.15 = (f32[128,1152]{1,0:T(8,128)S(1)}, f32[128,1152]{1,0:T(8,128)S(1)}, u32[]{:S(2)}, u32[]{:S(2)}) collective-permute-start(f32[128,1152]{1,0:T(8,128)S(1)} %concatenate.94), channel_id=1, source_target_pairs={{0,8},{2,10},{4,12},{6,14},{8,16},{10,18},{12,20},{14,22},{16,24},... | collective-permute-start | bytes 1769480 | tf_op jit(solution)/shard_map/ppermute | solution.py:11
  270.1 1.3 collective-permute-start.8
  271.6 6.4 %collective-permute-done.13 = f32[128,1152]{1,0:T(8,128)S(1)} collective-permute-done((f32[128,1152]{1,0:T(8,128)S(1)}, f32[128,1152]{1,0:T(8,128)S(1)}, u32[]{:S(2)}, u32[]{:S(2)}) %collective-permute-start.13) | collective-permute-done | bytes 589856 | tf_op jit(solution)/shard_map/ppermute | solution.py:11
  278.0 12.5 %collective-permute-done.14 = f32[128,1152]{1,0:T(8,128)S(1)} collective-permute-done((f32[128,1152]{1,0:T(8,128)S(1)}, f32[128,1152]{1,0:T(8,128)S(1)}, u32[]{:S(2)}, u32[]{:S(2)}) %collective-permute-start.14) | collective-permute-done | bytes 589856 | tf_op jit(solution)/shard_map/ppermute | solution.py:11
  290.5 21.3 %collective-permute-done.8 = f32[128,1152]{1,0:T(8,128)S(1)} collective-permute-done((f32[128,1152]{1,0:T(8,128)S(1)}, f32[128,1152]{1,0:T(8,128)S(1)}, u32[]{:S(2)}, u32[]{:S(2)}) %collective-permute-start.8) | collective-permute-done | bytes 589856 | tf_op jit(solution)/shard_map/ppermute | solution.py:11
  311.8 1.1 fusion.7
  313.0 10.4 %convolution_convert_fusion.1 = bf16[2048,1152]{1,0:T(8,128)(2,1)} fusion(bf16[2048,1152]{1,0:T(8,128)(2,1)} %bitcast.61, bf16[1152,1152]{1,0:T(8,128)(2,1)S(1)} %pad_dynamic-update-slice_fusion), kind=kOutput, calls=%fused_computation.3 | convolution fusion | flops 5438177280 | bytes 12091392 | tf_op jit(solution)/shard_map/dot_general | solution.py:58
  323.4 5.2 %reshape.72 = bf16[16,147456]{1,0:T(8,128)(2,1)} reshape(bf16[2048,1152]{1,0:T(8,128)(2,1)} %convolution_convert_fusion.1) | data formatting | bytes 9437184 | tf_op jit(solution)/shard_map/reshape | solution.py:59
  328.6 7.7 %fusion.18 = f32[16,32]{1,0:T(8,128)S(1)} fusion(bf16[16,147456]{1,0:T(8,128)(2,1)} %reshape.72, bf16[32,147456]{1,0:T(8,128)(2,1)} %bitcast.56), kind=kOutput, calls=%fused_computation.69 | convolution fusion | flops 150994944 | bytes 14157824 | tf_op jit(solution)/shard_map/dot_general | solution.py:68
  336.4 30.0 %psum.7 = f32[16,32]{1,0:T(8,128)S(1)} all-reduce(f32[16,32]{1,0:T(8,128)S(1)} %fusion.18), channel_id=1, replica_groups=mesh['chain'=16,'aux'=2] {'chain'}, use_global_device_ids=true, to_apply=%region_3.4 | all-reduce | flops 512 | bytes 4096 | tf_op jit(solution)/shard_map/psum | solution.py:74
  366.4 0.6 broadcast_multiply_fusion
  367.0 1.7 select_multiply_fusion
  (73 shorter events, 1.7 us)
Async XLA Ops:
  7.2 211.1 %copy-start = (bf16[16,32]{1,0:T(8,128)(2,1)S(1)}, bf16[16,32]{1,0:T(8,128)(2,1)}, u32[]{:S(2)}) copy-start(bf16[16,32]{1,0:T(8,128)(2,1)} %param.9) | copy-start | bytes 3076
  7.2 359.8 %reduce-scatter.2.cloned.1.call-start = ((), (), s32[]{:S(2)}) async-start(), calls=%async_computation.2 | async-start | bytes 884736 | tf_op jit(solution)/shard_map/reduce_scatter | solution.py:87
  11.3 18.7 %collective-permute-start = (bf16[2,128,1152]{2,1,0:T(8,128)(2,1)S(1)}, bf16[2,128,1152]{2,1,0:T(8,128)(2,1)S(1)}, u32[]{:S(2)}, u32[]{:S(2)}) collective-permute-start(bf16[2,128,1152]{2,1,0:T(8,128)(2,1)S(1)} %pad_maximum_fusion.1), channel_id=1, source_target_pairs={{0,8},{2,10},{4,12},{6,14},{8,16},{10,18},{12,20},{14,22},{16,24},... | collective-permute-start | bytes 1769480 | tf_op jit(solution)/shard_map/ppermute | solution.py:11
  16.3 15.0 %collective-permute-start.1 = (bf16[2,128,1152]{2,1,0:T(8,128)(2,1)S(1)}, bf16[2,128,1152]{2,1,0:T(8,128)(2,1)S(1)}, u32[]{:S(2)}, u32[]{:S(2)}) collective-permute-start(bf16[2,128,1152]{2,1,0:T(8,128)(2,1)S(1)} %pad_maximum_fusion.1), channel_id=1, source_target_pairs={{0,6},{2,8},{4,10},{6,12},{8,14},{10,16},{12,18},{14,20},{16,22},{... | collective-permute-start | bytes 1769480 | tf_op jit(solution)/shard_map/ppermute | solution.py:11
  18.9 48.1 %collective-permute-start.2 = (bf16[2,128,1152]{2,1,0:T(8,128)(2,1)S(1)}, bf16[2,128,1152]{2,1,0:T(8,128)(2,1)S(1)}, u32[]{:S(2)}, u32[]{:S(2)}) collective-permute-start(bf16[2,128,1152]{2,1,0:T(8,128)(2,1)S(1)} %pad_maximum_fusion.1), channel_id=1, source_target_pairs={{0,4},{2,6},{4,8},{6,10},{8,12},{10,14},{12,16},{14,18},{16,20},{1... | collective-permute-start | bytes 1769480 | tf_op jit(solution)/shard_map/ppermute | solution.py:11
  22.4 46.0 %collective-permute-start.3 = (bf16[2,128,1152]{2,1,0:T(8,128)(2,1)S(1)}, bf16[2,128,1152]{2,1,0:T(8,128)(2,1)S(1)}, u32[]{:S(2)}, u32[]{:S(2)}) collective-permute-start(bf16[2,128,1152]{2,1,0:T(8,128)(2,1)S(1)} %pad_maximum_fusion.1), channel_id=1, source_target_pairs={{0,2},{2,4},{4,6},{6,8},{8,10},{10,12},{12,14},{14,16},{16,18},{18... | collective-permute-start | bytes 1769480 | tf_op jit(solution)/shard_map/ppermute | solution.py:11
  25.0 43.5 %collective-permute-start.4 = (bf16[2,128,1152]{2,1,0:T(8,128)(2,1)S(1)}, bf16[2,128,1152]{2,1,0:T(8,128)(2,1)S(1)}, u32[]{:S(2)}, u32[]{:S(2)}) collective-permute-start(bf16[2,128,1152]{2,1,0:T(8,128)(2,1)S(1)} %pad_maximum_fusion.1), channel_id=1, source_target_pairs={{2,0},{4,2},{6,4},{8,6},{10,8},{12,10},{14,12},{16,14},{18,16},{20... | collective-permute-start | bytes 1769480 | tf_op jit(solution)/shard_map/ppermute | solution.py:11
  29.9 49.6 %copy-start.2 = (bf16[16,128,1152]{2,1,0:T(8,128)(2,1)}, bf16[16,128,1152]{2,1,0:T(8,128)(2,1)S(1)}, u32[]{:S(2)}) copy-start(bf16[16,128,1152]{2,1,0:T(8,128)(2,1)S(1)} %broadcast_select_fusion) | copy-start | bytes 14155780
  30.0 38.6 %collective-permute-start.5 = (bf16[2,128,1152]{2,1,0:T(8,128)(2,1)S(1)}, bf16[2,128,1152]{2,1,0:T(8,128)(2,1)S(1)}, u32[]{:S(2)}, u32[]{:S(2)}) collective-permute-start(bf16[2,128,1152]{2,1,0:T(8,128)(2,1)S(1)} %pad_maximum_fusion.1), channel_id=1, source_target_pairs={{4,0},{6,2},{8,4},{10,6},{12,8},{14,10},{16,12},{18,14},{20,16},{2... | collective-permute-start | bytes 1769480 | tf_op jit(solution)/shard_map/ppermute | solution.py:11
  31.3 37.3 %collective-permute-start.6 = (bf16[2,128,1152]{2,1,0:T(8,128)(2,1)S(1)}, bf16[2,128,1152]{2,1,0:T(8,128)(2,1)S(1)}, u32[]{:S(2)}, u32[]{:S(2)}) collective-permute-start(bf16[2,128,1152]{2,1,0:T(8,128)(2,1)S(1)} %pad_maximum_fusion.1), channel_id=1, source_target_pairs={{6,0},{8,2},{10,4},{12,6},{14,8},{16,10},{18,12},{20,14},{22,16},{... | collective-permute-start | bytes 1769480 | tf_op jit(solution)/shard_map/ppermute | solution.py:11
  67.1 11.8 %collective-permute-start.7 = (bf16[2,128,1152]{2,1,0:T(8,128)(2,1)S(1)}, bf16[2,128,1152]{2,1,0:T(8,128)(2,1)S(1)}, u32[]{:S(2)}, u32[]{:S(2)}) collective-permute-start(bf16[2,128,1152]{2,1,0:T(8,128)(2,1)S(1)} %pad_maximum_fusion.1), channel_id=1, source_target_pairs={{8,0},{10,2},{12,4},{14,6},{16,8},{18,10},{20,12},{22,14},{24,16},... | collective-permute-start | bytes 1769480 | tf_op jit(solution)/shard_map/ppermute | solution.py:11
  69.0 10.1 %copy-start.3 = (bf16[128,1152]{1,0:T(8,128)(2,1)S(1)}, bf16[128,1152]{1,0:T(8,128)(2,1)}, u32[]{:S(2)}) copy-start(bf16[128,1152]{1,0:T(8,128)(2,1)} %param.6) | copy-start | bytes 884740
  69.0 10.1 %copy-start.4 = (bf16[128,1152]{1,0:T(8,128)(2,1)S(1)}, bf16[128,1152]{1,0:T(8,128)(2,1)}, u32[]{:S(2)}) copy-start(bf16[128,1152]{1,0:T(8,128)(2,1)} %param.7) | copy-start | bytes 884740
  241.2 22.9 %collective-permute-start.11 = (f32[128,1152]{1,0:T(8,128)S(1)}, f32[128,1152]{1,0:T(8,128)S(1)}, u32[]{:S(2)}, u32[]{:S(2)}) collective-permute-start(f32[128,1152]{1,0:T(8,128)S(1)} %concatenate.90), channel_id=1, source_target_pairs={{2,0},{4,2},{6,4},{8,6},{10,8},{12,10},{14,12},{16,14},{18,16},{20... | collective-permute-start | bytes 1769480 | tf_op jit(solution)/shard_map/ppermute | solution.py:11
  242.5 22.9 %collective-permute-start.12 = (f32[128,1152]{1,0:T(8,128)S(1)}, f32[128,1152]{1,0:T(8,128)S(1)}, u32[]{:S(2)}, u32[]{:S(2)}) collective-permute-start(f32[128,1152]{1,0:T(8,128)S(1)} %concatenate.91), channel_id=1, source_target_pairs={{0,2},{2,4},{4,6},{6,8},{8,10},{10,12},{12,14},{14,16},{16,18},{18... | collective-permute-start | bytes 1769480 | tf_op jit(solution)/shard_map/ppermute | solution.py:11
  245.7 24.5 %collective-permute-start.10 = (f32[128,1152]{1,0:T(8,128)S(1)}, f32[128,1152]{1,0:T(8,128)S(1)}, u32[]{:S(2)}, u32[]{:S(2)}) collective-permute-start(f32[128,1152]{1,0:T(8,128)S(1)} %concatenate.89), channel_id=1, source_target_pairs={{4,0},{6,2},{8,4},{10,6},{12,8},{14,10},{16,12},{18,14},{20,16},{2... | collective-permute-start | bytes 1769480 | tf_op jit(solution)/shard_map/ppermute | solution.py:11
  247.0 31.0 %collective-permute-start.13 = (f32[128,1152]{1,0:T(8,128)S(1)}, f32[128,1152]{1,0:T(8,128)S(1)}, u32[]{:S(2)}, u32[]{:S(2)}) collective-permute-start(f32[128,1152]{1,0:T(8,128)S(1)} %concatenate.92), channel_id=1, source_target_pairs={{0,4},{2,6},{4,8},{6,10},{8,12},{10,14},{12,16},{14,18},{16,20},{1... | collective-permute-start | bytes 1769480 | tf_op jit(solution)/shard_map/ppermute | solution.py:11
  252.3 38.3 %collective-permute-start.14 = (f32[128,1152]{1,0:T(8,128)S(1)}, f32[128,1152]{1,0:T(8,128)S(1)}, u32[]{:S(2)}, u32[]{:S(2)}) collective-permute-start(f32[128,1152]{1,0:T(8,128)S(1)} %concatenate.93), channel_id=1, source_target_pairs={{0,6},{2,8},{4,10},{6,12},{8,14},{10,16},{12,18},{14,20},{16,22},{... | collective-permute-start | bytes 1769480 | tf_op jit(solution)/shard_map/ppermute | solution.py:11
  264.1 26.4 %collective-permute-start.9 = (f32[128,1152]{1,0:T(8,128)S(1)}, f32[128,1152]{1,0:T(8,128)S(1)}, u32[]{:S(2)}, u32[]{:S(2)}) collective-permute-start(f32[128,1152]{1,0:T(8,128)S(1)} %concatenate.88), channel_id=1, source_target_pairs={{6,0},{8,2},{10,4},{12,6},{14,8},{16,10},{18,12},{20,14},{22,16},{... | collective-permute-start | bytes 1769480 | tf_op jit(solution)/shard_map/ppermute | solution.py:11
  265.4 25.1 %collective-permute-start.15 = (f32[128,1152]{1,0:T(8,128)S(1)}, f32[128,1152]{1,0:T(8,128)S(1)}, u32[]{:S(2)}, u32[]{:S(2)}) collective-permute-start(f32[128,1152]{1,0:T(8,128)S(1)} %concatenate.94), channel_id=1, source_target_pairs={{0,8},{2,10},{4,12},{6,14},{8,16},{10,18},{12,20},{14,22},{16,24},... | collective-permute-start | bytes 1769480 | tf_op jit(solution)/shard_map/ppermute | solution.py:11
  270.1 41.7 %collective-permute-start.8 = (f32[128,1152]{1,0:T(8,128)S(1)}, f32[128,1152]{1,0:T(8,128)S(1)}, u32[]{:S(2)}, u32[]{:S(2)}) collective-permute-start(f32[128,1152]{1,0:T(8,128)S(1)} %concatenate.87), channel_id=1, source_target_pairs={{8,0},{10,2},{12,4},{14,6},{16,8},{18,10},{20,12},{22,14},{24,16},... | collective-permute-start | bytes 1769480 | tf_op jit(solution)/shard_map/ppermute | solution.py:11
  328.6 40.0 %copy-start.1 = (bf16[16,32]{1,0:T(8,128)(2,1)S(1)}, bf16[16,32]{1,0:T(8,128)(2,1)}, u32[]{:S(2)}) copy-start(bf16[16,32]{1,0:T(8,128)(2,1)} %param.9) | copy-start | bytes 3076
Sparse Core Ops, SparseCore 0:
  313.1 17.8 reduce-scatter.1
